TPU v7x, 32 devices: a whole 2x2x4 slice. The times are simulated.
32 devices in a mesh: row: 4 (over y, x), col: 8 (over z, core).
Axes of the slice: x: 2, y: 2, z: 4, core: 2. Of those that a mesh axis runs over, the one named last changes fastest.
Arguments:
- noise: float32 [2048, 3072], P('row', 'col'), may hold values from -30 to 30
- images: float32 [6144, 3072], P('col', 'row'), may hold values from -6 to 6
- time_index: int32 [2048], P('row'), may hold values from 0 to 999
- w_in: float32 [3072, 3072], P(None, 'col'), may hold values from -0.109375 to 0.109375
- time_gain: float32 [3072], P('col'), may hold values from -5 to 5
- w_out: float32 [3072, 3072], P('col'), may hold values from -0.109375 to 0.109375
Outputs:
- targets: float32 [2048, 3072], P('row', 'col')
- row_pot: float32 [2048], P('row')
- col_pot: float32 [6144], P('col')
- grad_in: float32 [3072, 3072], P('row', 'col')
- grad_time: float32 [3072], P('col')
- grad_out: float32 [3072, 3072], P('col', 'row')
- mse: float32 [], replicated
All inputs are finite; a program needn't handle non-finite values.
Results may differ from a plain program's by a relative error of at most 0.0003.
Values sent between devices are 32-bit elements; how exact they have to be, the bound alone decides.
A program may use at most 128 MiB of HBM per device.

v0:
```python
import jax
import jax.numpy as jnp
from jax import lax
from jax.sharding import PartitionSpec as P

ITERS = 2
TIMES = 1000
EPSILON = 0.01


def merged(array, axis, combine):
    everything = jax.tree.map(lambda part: lax.all_gather(part, axis), array)
    first = jax.tree.map(lambda part: part[0], everything)

    def hop(k, so_far):
        return combine(so_far, jax.tree.map(lambda part: part[k], everything))

    return lax.fori_loop(1, lax.axis_size(axis), hop, first)


def joined(left_pair, right_pair):
    peak = jnp.maximum(left_pair[0], right_pair[0])
    total = left_pair[1] * jnp.exp(left_pair[0] - peak) + right_pair[1] * jnp.exp(
        right_pair[0] - peak
    )
    return (peak, total)


def over_images(logits):
    local_peak = jnp.max(logits, axis=1)
    local_total = jnp.sum(jnp.exp(logits - local_peak[:, None]), axis=1)
    peak, total = merged((local_peak, local_total), "col", joined)
    return (peak, total)


def over_noise(logits):
    local_peak = jnp.max(logits, axis=0)
    local_total = jnp.sum(jnp.exp(logits - local_peak[None, :]), axis=0)
    peak, total = merged((local_peak, local_total), "row", joined)
    return (peak, total)


def body(noise, images, time_index, w_in, time_gain, w_out):
    highest = lax.Precision.HIGHEST
    full_noise = lax.all_gather(noise, "col", axis=1, tiled=True)
    full_images = lax.all_gather(images, "row", axis=1, tiled=True)
    width = full_noise.shape[1]
    noise_count = full_noise.shape[0] * lax.axis_size("row")
    image_count = full_images.shape[0] * lax.axis_size("col")
    noise_norms = jnp.sum(full_noise * full_noise, axis=1)
    image_norms = jnp.sum(full_images * full_images, axis=1)
    cross = lax.dot_general(
        full_noise,
        full_images,
        (((1,), (1,)), ((), ())),
        precision=highest,
        preferred_element_type=jnp.float32,
    )
    scaled = (noise_norms[:, None] + image_norms[None, :] - 2.0 * cross) / (width * EPSILON)
    col_pot = jnp.zeros((full_images.shape[0],), jnp.float32)
    row_pot = jnp.zeros((full_noise.shape[0],), jnp.float32)
    for iteration in range(ITERS):
        peak, total = over_images(col_pot[None, :] - scaled)
        row_pot = jnp.log(jnp.float32(image_count)) - (jnp.log(total) + peak)
        peak, total = over_noise(row_pot[:, None] - scaled)
        col_pot = jnp.log(jnp.float32(noise_count)) - (jnp.log(total) + peak)
    logits = col_pot[None, :] - scaled
    peak, total = over_images(logits)
    weights = jnp.exp(logits - (jnp.log(total) + peak)[:, None])
    partial_value = jnp.dot(
        weights, full_images, precision=highest, preferred_element_type=jnp.float32
    )
    slice_width = noise.shape[1]
    slice_start = lax.axis_index("col") * slice_width
    whole_targets = lax.psum(partial_value, "col")
    targets = lax.dynamic_slice_in_dim(whole_targets, slice_start, slice_width, 1)
    fraction = (time_index.astype(jnp.float32) + 0.5) / TIMES
    mixed = (1.0 - fraction)[:, None] * full_noise + fraction[:, None] * whole_targets
    velocity = whole_targets - full_noise
    pre = (
        jnp.dot(mixed, w_in, precision=highest, preferred_element_type=jnp.float32)
        + fraction[:, None] * time_gain[None, :]
    )
    sigma = jax.nn.sigmoid(pre)
    hidden = pre * sigma
    part_out = jnp.dot(hidden, w_out, precision=highest, preferred_element_type=jnp.float32)
    out = lax.psum(part_out, "col")
    diff = out - velocity
    squared = jnp.sum(diff * diff)
    slope = diff / jnp.sqrt(jnp.float32(noise_count))
    local_out = lax.dot_general(
        hidden,
        slope,
        (((0,), (0,)), ((), ())),
        precision=highest,
        preferred_element_type=jnp.float32,
    )
    back = lax.dot_general(
        slope,
        w_out,
        (((1,), (1,)), ((), ())),
        precision=highest,
        preferred_element_type=jnp.float32,
    )
    dpre = back * sigma * (1.0 + pre * (1.0 - sigma))
    local_in = lax.dot_general(
        mixed, dpre, (((0,), (0,)), ((), ())), precision=highest, preferred_element_type=jnp.float32
    )
    local_time = jnp.sum(fraction[:, None] * dpre, axis=0)
    grad_in, grad_out = (
        lax.psum_scatter(local_in, "row", scatter_dimension=0, tiled=True),
        lax.psum_scatter(local_out, "row", scatter_dimension=1, tiled=True),
    )
    grad_time, squared_all = lax.psum((local_time, squared), "row")
    mse = squared_all / (noise_count * width)
    return (targets, row_pot, col_pot, grad_in, grad_time, grad_out, mse)


def solution(mesh):
    placed = (P("row", "col"), P("col", "row"), P("row"), P(None, "col"), P("col"), P("col", None))
    return jax.shard_map(
        body,
        mesh=mesh,
        in_specs=placed,
        out_specs=(
            P("row", "col"),
            P("row"),
            P("col"),
            P("row", "col"),
            P("col"),
            P("col", "row"),
            P(),
        ),
        check_vma=False,
    )
```

profile of v0, /device:TPU:0, one launch (start us, length us, event | category | flops | bytes accessed | tf_op | source)
XLA Modules:
  0.0 786.1 jit_solution(18099109052659360453)
XLA Ops:
  7.2 0.7 all-gather.23.cloned.1.call-update
  7.9 0.7 all-gather.25.cloned.1.call-update
  8.7 68.3 %all-gather.23.cloned.1.call-done = f32[512,3072]{1,0:T(8,128)} async-done(((f32[512,384]{1,0:T(8,128)}), f32[512,3072]{1,0:T(8,128)}) %all-gather.23.cloned.1.call-update) | async-done | bytes 6291472 | tf_op jit(solution)/shard_map/all_gather | solution.py:45
  77.0 3.3 multiply_reduce_fusion.2
  80.3 93.5 %all-gather.25.cloned.1.call-done = f32[768,3072]{1,0:T(8,128)} async-done(((f32[768,768]{1,0:T(8,128)}), f32[768,3072]{1,0:T(8,128)}) %all-gather.25.cloned.1.call-update) | async-done | bytes 9437200 | tf_op jit(solution)/shard_map/all_gather | solution.py:46
  173.8 4.5 multiply_reduce_fusion
  178.3 1.0 copy-done
  179.2 18.3 %subtract_reduce_fusion.3 = (f32[512]{0:T(512)S(1)}, f32[512,768]{1,0:T(8,128)S(1)}) fusion(f32[512,3072]{1,0:T(8,128)S(1)} %copy-done, f32[768,3072]{1,0:T(8,128)} %all-gather.25.cloned.1.call-done, f32[768]{0:T(1024)S(1)} %multiply_reduce_fusion, f32[512]{0:T(512)S(1)} %multiply_reduce_fusion.2), kind=kOutput, calls=%fused_computation.38 | convolution fusion | flops 14497873920 | bytes 17308672 | tf_op jit(solution)/shard_map/dot_general | solution.py:52
  197.5 0.4 exponential_reduce_fusion.4
  197.9 12.8 %all-gather.11 = f32[8,1,512]{2,1,0:T(1,128)S(1)} all-gather(f32[1,1,512]{2,1,0:T(1,128)S(1)} %bitcast.95), channel_id=3, replica_groups=mesh['row'=4,'col'=8] {'col'}, dimensions={0}, use_global_device_ids=true | all-gather | bytes 18432 | tf_op jit(solution)/shard_map/all_gather | solution.py:12
  210.8 12.8 %all-gather.10 = f32[8,1,512]{2,1,0:T(1,128)S(1)} all-gather(f32[1,1,512]{2,1,0:T(1,128)S(1)} %bitcast.93), channel_id=2, replica_groups=mesh['row'=4,'col'=8] {'col'}, dimensions={0}, use_global_device_ids=true | all-gather | bytes 18432 | tf_op jit(solution)/shard_map/all_gather | solution.py:12
  223.5 0.4 while.85
  224.1 0.3 exponential_reduce_fusion.3
  224.5 8.1 %all-gather.13 = f32[4,1,768]{2,1,0:T(1,128)S(1)} all-gather(f32[1,1,768]{2,1,0:T(1,128)S(1)} %reshape.65), channel_id=5, replica_groups=mesh['row'=4,'col'=8] {'row'}, dimensions={0}, use_global_device_ids=true | all-gather | bytes 15360 | tf_op jit(solution)/shard_map/all_gather | solution.py:12
  232.6 7.2 all-gather.12
  239.9 0.2 while.86
  240.3 0.4 exponential_reduce_fusion.2
  240.7 12.8 %all-gather.15 = f32[8,1,512]{2,1,0:T(1,128)S(1)} all-gather(f32[1,1,512]{2,1,0:T(1,128)S(1)} %bitcast.94), channel_id=7, replica_groups=mesh['row'=4,'col'=8] {'col'}, dimensions={0}, use_global_device_ids=true | all-gather | bytes 18432 | tf_op jit(solution)/shard_map/all_gather | solution.py:12
  253.5 12.8 %all-gather.14 = f32[8,1,512]{2,1,0:T(1,128)S(1)} all-gather(f32[1,1,512]{2,1,0:T(1,128)S(1)} %bitcast.91), channel_id=6, replica_groups=mesh['row'=4,'col'=8] {'col'}, dimensions={0}, use_global_device_ids=true | all-gather | bytes 18432 | tf_op jit(solution)/shard_map/all_gather | solution.py:12
  266.3 0.4 while.87
  266.9 0.3 exponential_reduce_fusion.1
  267.2 8.1 %all-gather.17 = f32[4,1,768]{2,1,0:T(1,128)S(1)} all-gather(f32[1,1,768]{2,1,0:T(1,128)S(1)} %reshape.73), channel_id=9, replica_groups=mesh['row'=4,'col'=8] {'row'}, dimensions={0}, use_global_device_ids=true | all-gather | bytes 15360 | tf_op jit(solution)/shard_map/all_gather | solution.py:12
  275.4 18.3 %all-gather.16 = f32[4,1,768]{2,1,0:T(1,128)S(1)} all-gather(f32[1,1,768]{2,1,0:T(1,128)S(1)} %reshape.71), channel_id=8, replica_groups=mesh['row'=4,'col'=8] {'row'}, dimensions={0}, use_global_device_ids=true | all-gather | bytes 15360 | tf_op jit(solution)/shard_map/all_gather | solution.py:12
  293.7 0.2 while.88
  293.9 0.2 subtract_reduce_fusion.4
  294.1 0.4 exponential_reduce_fusion
  294.6 12.8 %all-gather.19 = f32[8,1,512]{2,1,0:T(1,128)S(1)} all-gather(f32[1,1,512]{2,1,0:T(1,128)S(1)} %bitcast.96), channel_id=11, replica_groups=mesh['row'=4,'col'=8] {'col'}, dimensions={0}, use_global_device_ids=true | all-gather | bytes 18432 | tf_op jit(solution)/shard_map/all_gather | solution.py:12
  307.3 12.8 %all-gather.18 = f32[8,1,512]{2,1,0:T(1,128)S(1)} all-gather(f32[1,1,512]{2,1,0:T(1,128)S(1)} %bitcast.92), channel_id=10, replica_groups=mesh['row'=4,'col'=8] {'col'}, dimensions={0}, use_global_device_ids=true | all-gather | bytes 18432 | tf_op jit(solution)/shard_map/all_gather | solution.py:12
  320.1 0.4 while.89
  320.5 19.3 %fusion.6 = f32[512,3072]{1,0:T(8,128)} fusion(f32[768,3072]{1,0:T(8,128)} %all-gather.25.cloned.1.call-done, f32[512,768]{1,0:T(8,128)S(1)} %get-tuple-element.759, f32[512]{0:T(512)S(1)} %log_add_fusion, f32[768]{0:T(1024)S(1)} %add_subtract_fusion), kind=kOutput, calls=%fused_computation.26 | convolution fusion | flops 14496301056 | bytes 17306624 | tf_op jit(solution)/shard_map/dot_general | solution.py:70
  339.9 0.6 copy-done.6
  340.4 133.1 %all-reduce.4.cloned.1.call-done = f32[512,3072]{1,0:T(8,128)} async-done(((f32[512,3072]{1,0:T(8,128)}), f32[512,3072]{1,0:T(8,128)}) %all-reduce.4.cloned.1.call-update) | async-done | bytes 6291472 | tf_op jit(solution)/shard_map/psum | solution.py:75
  473.6 14.6 %convolution_add_fusion = f32[512,384]{1,0:T(8,128)S(1)} fusion(f32[3072,384]{1,0:T(8,128)} %param.19, f32[384]{0:T(512)S(1)} %copy-done.7, f32[512]{0:T(512)S(1)} %get-tuple-element.757, f32[512,3072]{1,0:T(8,128)} %all-reduce.4.cloned.1.call-done, f32[512,3072]{1,0:T(8,128)} %all-gather.23.cloned.1.call-done, f32[512]{0:T(512)S(1)} %get-tuple-element.756), kind=kOutput, calls=%fused_computation.43 | convolution fusion | flops 7252869120 | bytes 18093568 | tf_op jit(solution)/shard_map/dot_general | solution.py:81
  488.2 0.9 copy-done.2
  489.1 12.0 %fusion.20 = f32[512,3072]{1,0:T(8,128)} fusion(f32[384,3072]{1,0:T(8,128)S(1)} %bitcast.68, f32[512,384]{1,0:T(8,128)S(1)} %convolution_add_fusion), kind=kOutput, calls=%fused_computation.49 | convolution fusion | flops 7248543744 | bytes 11796480 | tf_op jit(solution)/shard_map/dot_general | solution.py:86
  501.1 0.3 reduce-scatter.5.cloned.1.call-start
  501.4 136.0 %all-reduce.6.cloned.1.call-done = f32[512,3072]{1,0:T(8,128)} async-done(((f32[512,3072]{1,0:T(8,128)}), f32[512,3072]{1,0:T(8,128)}) %all-reduce.6.cloned.1.call-update) | async-done | bytes 6291472 | tf_op jit(solution)/shard_map/psum | solution.py:87
  637.3 9.5 %multiply_reduce_fusion.1 = (f32[]{:T(128)}, f32[512,3072]{1,0:T(8,128)S(1)}) fusion(f32[512,3072]{1,0:T(8,128)} %all-reduce.6.cloned.1.call-done, f32[512,3072]{1,0:T(8,128)} %all-reduce.4.cloned.1.call-done, f32[512,3072]{1,0:T(8,128)} %all-gather.23.cloned.1.call-done), kind=kLoop, calls=%fused_computation.16 | loop fusion | flops 6291455 | bytes 25165828 | tf_op jit(solution)/shard_map/reduce_sum | solution.py:89
  646.8 2.6 copy-done.1
  649.4 10.6 %fusion = f32[384,3072]{1,0:T(8,128)} fusion(f32[512,3072]{1,0:T(8,128)S(1)} %get-tuple-element.745, f32[512,384]{1,0:T(8,128)} %copy-done.2), kind=kOutput, calls=%fused_computation.20 | convolution fusion | flops 7250116608 | bytes 11796480 | tf_op jit(solution)/shard_map/dot_general | solution.py:91
  660.1 0.3 reduce-scatter.3.cloned.1.call-start
  660.4 0.8 copy-done.3
  661.2 14.1 %multiply_reduce_fusion.3 = (f32[384]{0:T(512)S(1)}, f32[512,384]{1,0:T(8,128)S(1)}) fusion(f32[512]{0:T(512)S(1)} %get-tuple-element.757, f32[512,384]{1,0:T(8,128)S(1)} %copy-done.3, f32[384,3072]{1,0:T(8,128)} %param.21, f32[512,3072]{1,0:T(8,128)} %copy-done.1), kind=kOutput, calls=%fused_computation.44 | convolution fusion | flops 7251295744 | bytes 12586496 | tf_op jit(solution)/shard_map/dot_general | solution.py:98
  675.3 15.4 %fusion.26 = f32[3072,384]{1,0:T(8,128)} fusion(f32[512,384]{1,0:T(8,128)S(1)} %get-tuple-element.761, f32[512,3072]{1,0:T(8,128)} %all-reduce.4.cloned.1.call-done, f32[512,3072]{1,0:T(8,128)} %all-gather.23.cloned.1.call-done, f32[512]{0:T(512)S(1)} %get-tuple-element.757, f32[512]{0:T(512)S(1)} %get-tuple-element.756), kind=kOutput, calls=%fused_computation.76 | convolution fusion | flops 7252475904 | bytes 18092032 | tf_op jit(solution)/shard_map/dot_general | solution.py:106
  690.7 2.1 constant_dynamic-slice_fusion.6
  692.8 10.5 %all-reduce = (f32[384]{0:T(512)}, f32[]{:T(128)}) all-reduce(f32[384]{0:T(512)S(1)} %get-tuple-element.760, f32[]{:T(128)} %get-tuple-element.744), channel_id=1, replica_groups=mesh['row'=4,'col'=8] {'row'}, use_global_device_ids=true, to_apply=%region_26.0 | all-reduce | flops 385 | bytes 3080 | tf_op jit(solution)/shard_map/psum | solution.py:114
  703.9 13.4 %reduce-scatter.5.cloned.1.call-done = f32[384,768]{1,0:T(8,128)} async-done(((f32[384,3072]{1,0:T(8,128)}), f32[384,768]{1,0:T(8,128)}) %reduce-scatter.5.cloned.1.call-update) | async-done | bytes 1179664 | tf_op jit(solution)/shard_map/reduce_scatter | solution.py:112
  717.3 60.4 %reduce-scatter.3.cloned.1.call-done = f32[768,384]{1,0:T(8,128)} async-done(((f32[3072,384]{1,0:T(8,128)}), f32[768,384]{1,0:T(8,128)}) %reduce-scatter.3.cloned.1.call-update) | async-done | bytes 1179664 | tf_op jit(solution)/shard_map/reduce_scatter | solution.py:111
  (111 shorter events, 1.8 us)
Async XLA Ops:
  7.2 69.9 %all-gather.23.cloned.1.call-start = ((), (), s32[]{:S(2)}) async-start(), calls=%async_computation.2 | async-start | bytes 7077888 | tf_op jit(solution)/shard_map/all_gather | solution.py:45
  7.9 165.9 %all-gather.25.cloned.1.call-start = ((), (), s32[]{:S(2)}) async-start(), calls=%async_computation.3 | async-start | bytes 11796480 | tf_op jit(solution)/shard_map/all_gather | solution.py:46
  8.6 464.9 %all-reduce.4.cloned.1.call-start = ((), (), s32[]{:S(2)}) async-start(), calls=%async_computation.4 | async-start | bytes 12582912 | tf_op jit(solution)/shard_map/psum | solution.py:75
  173.8 5.5 copy-start
  266.7 73.1 %copy-start.5 = (f32[512]{0:T(512)}, f32[512]{0:T(512)S(1)}, u32[]{:S(2)}) copy-start(f32[512]{0:T(512)S(1)} %add_subtract_fusion.2) | copy-start | bytes 6148
  293.9 45.8 %copy-start.4 = (f32[768]{0:T(1024)}, f32[768]{0:T(1024)S(1)}, u32[]{:S(2)}) copy-start(f32[768]{0:T(1024)S(1)} %add_subtract_fusion) | copy-start | bytes 9220
  339.8 0.7 copy-start.6
  339.8 133.8 %copy-start.7 = (f32[384]{0:T(512)S(1)}, f32[384]{0:T(512)}, u32[]{:S(2)}) copy-start(f32[384]{0:T(512)} %param.20) | copy-start | bytes 4612
  339.8 149.3 %slice-start = ((s8[4718592]{0:T(1024)(128)(4,1)}), s8[524288]{0:T(1024)(128)(4,1)S(1)}, s32[]{:S(2)}) async-start(s8[4718592]{0:T(1024)(128)(4,1)} %bitcast.67), calls=%async_computation.8 | async-start | bytes 1048576
  339.8 297.5 %all-reduce.6.cloned.1.call-start = ((), (), s32[]{:S(2)}) async-start(), calls=%async_computation.5 | async-start | bytes 12582912 | tf_op jit(solution)/shard_map/psum | solution.py:87
  473.6 15.5 %slice-start.1 = ((s8[4718592]{0:T(1024)(128)(4,1)}), s8[4194304]{0:T(1024)(128)(4,1)S(1)}, s32[]{:S(2)}) async-start(s8[4718592]{0:T(1024)(128)(4,1)} %bitcast.67), calls=%async_computation.9 | async-start | bytes 8388608
  488.2 0.9 copy-start.2
  501.1 216.2 %reduce-scatter.5.cloned.1.call-start = ((), (), s32[]{:S(2)}) async-start(), calls=%async_computation.7 | async-start | bytes 5898240 | tf_op jit(solution)/shard_map/reduce_scatter | solution.py:112
  646.8 2.6 copy-start.1
  660.1 1.1 copy-start.3
  660.1 117.6 %reduce-scatter.3.cloned.1.call-start = ((), (), s32[]{:S(2)}) async-start(), calls=%async_computation.6 | async-start | bytes 5898240 | tf_op jit(solution)/shard_map/reduce_scatter | solution.py:111
Sparse Core Ops, SparseCore 0:
  9.6 67.4 all-gather.22
  78.9 94.8 all-gather.24
  339.9 133.6 all-reduce.3
  501.2 136.0 all-reduce.5
  660.2 57.0 reduce-scatter.4
  720.7 56.9 reduce-scatter.2
where the time goes:
time: 794 us; the launch traced here: 786 us
  waiting for transfers between devices  506 us (64%)
  blocking collectives  129 us (16%)
  matrix products  104 us (13%)
  other arithmetic  20.5 us (3%)
  between operations  16.6 us (2%)
  local copies, waits for them, and re-layouts  8.41 us (1%)
    psum x1, waiting for transfers between devices, body(): out = lax.psum(part_out, 'col')  136 us
    psum x1, waiting for transfers between devices, body(): whole_targets = lax.psum(partial_value, 'col')  133 us
    all_gather x10, blocking collectives, merged(): everything = jax.tree.map(lambda part: lax.all_gather(part, axis), array)  118 us
    all_gather x1, waiting for transfers between devices, body(): full_images = lax.all_gather(images, 'row', axis=1, tiled=True)  93.5 us
    all_gather x1, waiting for transfers between devices, body(): full_noise = lax.all_gather(noise, 'col', axis=1, tiled=True)  68.3 us
    reduce_scatter x1, waiting for transfers between devices, body(): lax.psum_scatter(local_in, 'row', scatter_dimension=0, tiled=True)  60.4 us
    dot_general x1, matrix products, body(): jnp.dot(weights, full_images, precision=highest, preferred_element_type=j...  19.3 us
    dot_general x1, matrix products, body(): lax.dot_general(full_noise, full_images, (((1,), (1,)), ((), ())), precis...  18.3 us
  transfers between devices with their start and end apart: 6, of which 6 were waited for; matrix products, arithmetic and copies ran while one was open for 4% of the time, Pallas kernels for 0%

commit v1 on v0

--- a/solution.py
+++ b/solution.py
@@ -84,7 +84,7 @@
     sigma = jax.nn.sigmoid(pre)
     hidden = pre * sigma
     part_out = jnp.dot(hidden, w_out, precision=highest, preferred_element_type=jnp.float32)
-    out = lax.psum(part_out, "col")
+    out = jnp.sum(lax.all_gather(part_out, "col"), axis=0)
     diff = out - velocity
     squared = jnp.sum(diff * diff)
     slope = diff / jnp.sqrt(jnp.float32(noise_count))

time: 794 us -> 1110 us (1.40)
  waiting for transfers between devices: 506 us -> 797 us
  other arithmetic: 20.5 us -> 44.9 us
    all_gather x0 -> x1, waiting for transfers between devices: none -> 427 us  [body(): out = jnp.sum(lax.all_gather(part_out, 'col'), axis=0)]
    psum x1 -> x0, waiting for transfers between devices: 136 us -> none  [body(): out = lax.psum(part_out, 'col')]
    reduce_sum x0 -> x1, other arithmetic: none -> 21.2 us  [body(): out = jnp.sum(lax.all_gather(part_out, 'col'), axis=0)]
  transfers between devices with their start and end apart: 6 -> 6, of which waited for: 6 -> 6; matrix products, arithmetic and copies ran while one was open for 4% -> 3% of each run, Pallas kernels for 0% -> 0%
where the time goes in v1:
time: 1110 us; the launch traced here: 1100 us
  waiting for transfers between devices  797 us (72%)
  blocking collectives  129 us (12%)
  matrix products  105 us (9%)
  other arithmetic  44.9 us (4%)
  between operations  16.6 us (1%)
    all_gather x1, waiting for transfers between devices, body(): out = jnp.sum(lax.all_gather(part_out, 'col'), axis=0)  427 us
    psum x1, waiting for transfers between devices, body(): whole_targets = lax.psum(partial_value, 'col')  133 us
    all_gather x10, blocking collectives, merged(): everything = jax.tree.map(lambda part: lax.all_gather(part, axis), array)  118 us
    all_gather x1, waiting for transfers between devices, body(): full_images = lax.all_gather(images, 'row', axis=1, tiled=True)  93.5 us
    all_gather x1, waiting for transfers between devices, body(): full_noise = lax.all_gather(noise, 'col', axis=1, tiled=True)  68.3 us
    reduce_scatter x1, waiting for transfers between devices, body(): lax.psum_scatter(local_in, 'row', scatter_dimension=0, tiled=True)  60.4 us
  transfers between devices with their start and end apart: 6, of which 6 were waited for; matrix products, arithmetic and copies ran while one was open for 3% of the time, Pallas kernels for 0%

profile of v1, /device:TPU:0, one launch (start us, length us, event | category | flops | bytes accessed | tf_op | source)
XLA Modules:
  0.0 1097.2 jit_solution(392495603078592700)
XLA Ops:
  7.2 0.7 all-gather.25.cloned.1.call-update
  7.9 0.7 all-gather.27.cloned.1.call-update
  8.7 68.3 %all-gather.25.cloned.1.call-done = f32[512,3072]{1,0:T(8,128)} async-done(((f32[512,384]{1,0:T(8,128)}), f32[512,3072]{1,0:T(8,128)}) %all-gather.25.cloned.1.call-update) | async-done | bytes 6291472 | tf_op jit(solution)/shard_map/all_gather | solution.py:45
  77.0 3.3 multiply_reduce_fusion.2
  80.3 93.5 %all-gather.27.cloned.1.call-done = f32[768,3072]{1,0:T(8,128)} async-done(((f32[768,768]{1,0:T(8,128)}), f32[768,3072]{1,0:T(8,128)}) %all-gather.27.cloned.1.call-update) | async-done | bytes 9437200 | tf_op jit(solution)/shard_map/all_gather | solution.py:46
  173.8 4.5 multiply_reduce_fusion
  178.3 1.0 copy-done
  179.2 18.3 %subtract_reduce_fusion.3 = (f32[512]{0:T(512)S(1)}, f32[512,768]{1,0:T(8,128)S(1)}) fusion(f32[512,3072]{1,0:T(8,128)S(1)} %copy-done, f32[768,3072]{1,0:T(8,128)} %all-gather.27.cloned.1.call-done, f32[768]{0:T(1024)S(1)} %multiply_reduce_fusion, f32[512]{0:T(512)S(1)} %multiply_reduce_fusion.2), kind=kOutput, calls=%fused_computation.38 | convolution fusion | flops 14497873920 | bytes 17308672 | tf_op jit(solution)/shard_map/dot_general | solution.py:52
  197.5 0.4 exponential_reduce_fusion.4
  197.9 12.8 %all-gather.12 = f32[8,1,512]{2,1,0:T(1,128)S(1)} all-gather(f32[1,1,512]{2,1,0:T(1,128)S(1)} %bitcast.97), channel_id=3, replica_groups=mesh['row'=4,'col'=8] {'col'}, dimensions={0}, use_global_device_ids=true | all-gather | bytes 18432 | tf_op jit(solution)/shard_map/all_gather | solution.py:12
  210.8 12.8 %all-gather.11 = f32[8,1,512]{2,1,0:T(1,128)S(1)} all-gather(f32[1,1,512]{2,1,0:T(1,128)S(1)} %bitcast.95), channel_id=2, replica_groups=mesh['row'=4,'col'=8] {'col'}, dimensions={0}, use_global_device_ids=true | all-gather | bytes 18432 | tf_op jit(solution)/shard_map/all_gather | solution.py:12
  223.5 0.4 while.85
  223.9 0.2 subtract_reduce_fusion.2
  224.1 0.3 exponential_reduce_fusion.3
  224.5 8.1 all-gather.14
  232.6 7.2 all-gather.13
  239.9 0.2 while.86
  240.1 0.2 subtract_reduce_fusion.1
  240.3 0.4 exponential_reduce_fusion.2
  240.7 12.8 %all-gather.16 = f32[8,1,512]{2,1,0:T(1,128)S(1)} all-gather(f32[1,1,512]{2,1,0:T(1,128)S(1)} %bitcast.96), channel_id=7, replica_groups=mesh['row'=4,'col'=8] {'col'}, dimensions={0}, use_global_device_ids=true | all-gather | bytes 18432 | tf_op jit(solution)/shard_map/all_gather | solution.py:12
  253.5 12.8 %all-gather.15 = f32[8,1,512]{2,1,0:T(1,128)S(1)} all-gather(f32[1,1,512]{2,1,0:T(1,128)S(1)} %bitcast.93), channel_id=6, replica_groups=mesh['row'=4,'col'=8] {'col'}, dimensions={0}, use_global_device_ids=true | all-gather | bytes 18432 | tf_op jit(solution)/shard_map/all_gather | solution.py:12
  266.3 0.4 while.87
  266.8 0.3 exponential_reduce_fusion.1
  267.2 8.1 all-gather.18
  275.4 18.3 %all-gather.17 = f32[4,1,768]{2,1,0:T(1,128)S(1)} all-gather(f32[1,1,768]{2,1,0:T(1,128)S(1)} %reshape.72), channel_id=8, replica_groups=mesh['row'=4,'col'=8] {'row'}, dimensions={0}, use_global_device_ids=true | all-gather | bytes 15360 | tf_op jit(solution)/shard_map/all_gather | solution.py:12
  293.7 0.2 while.88
  293.9 0.2 subtract_reduce_fusion.4
  294.1 0.4 exponential_reduce_fusion
  294.5 12.8 %all-gather.20 = f32[8,1,512]{2,1,0:T(1,128)S(1)} all-gather(f32[1,1,512]{2,1,0:T(1,128)S(1)} %bitcast.98), channel_id=11, replica_groups=mesh['row'=4,'col'=8] {'col'}, dimensions={0}, use_global_device_ids=true | all-gather | bytes 18432 | tf_op jit(solution)/shard_map/all_gather | solution.py:12
  307.3 12.8 %all-gather.19 = f32[8,1,512]{2,1,0:T(1,128)S(1)} all-gather(f32[1,1,512]{2,1,0:T(1,128)S(1)} %bitcast.94), channel_id=10, replica_groups=mesh['row'=4,'col'=8] {'col'}, dimensions={0}, use_global_device_ids=true | all-gather | bytes 18432 | tf_op jit(solution)/shard_map/all_gather | solution.py:12
  320.1 0.4 while.89
  320.5 19.3 %fusion.6 = f32[512,3072]{1,0:T(8,128)} fusion(f32[768,3072]{1,0:T(8,128)} %all-gather.27.cloned.1.call-done, f32[512,768]{1,0:T(8,128)S(1)} %get-tuple-element.759, f32[512]{0:T(512)S(1)} %log_add_fusion, f32[768]{0:T(1024)S(1)} %add_subtract_fusion), kind=kOutput, calls=%fused_computation.26 | convolution fusion | flops 14496301056 | bytes 17306624 | tf_op jit(solution)/shard_map/dot_general | solution.py:70
  339.8 0.6 copy-done.3
  340.4 133.1 %all-reduce.3.cloned.1.call-done = f32[512,3072]{1,0:T(8,128)} async-done(((f32[512,3072]{1,0:T(8,128)}), f32[512,3072]{1,0:T(8,128)}) %all-reduce.3.cloned.1.call-update) | async-done | bytes 6291472 | tf_op jit(solution)/shard_map/psum | solution.py:75
  473.6 14.5 %convolution_add_fusion = f32[512,384]{1,0:T(8,128)S(1)} fusion(f32[3072,384]{1,0:T(8,128)} %param.19, f32[384]{0:T(512)S(1)} %copy-done.4, f32[512]{0:T(512)S(1)} %get-tuple-element.757, f32[512,3072]{1,0:T(8,128)} %all-reduce.3.cloned.1.call-done, f32[512,3072]{1,0:T(8,128)} %all-gather.25.cloned.1.call-done, f32[512]{0:T(512)S(1)} %get-tuple-element.756), kind=kOutput, calls=%fused_computation.43 | convolution fusion | flops 7252869120 | bytes 18093568 | tf_op jit(solution)/shard_map/dot_general | solution.py:81
  488.1 12.0 %fusion.20 = f32[512,3072]{1,0:T(8,128)} fusion(f32[384,3072]{1,0:T(8,128)S(1)} %bitcast.70, f32[512,384]{1,0:T(8,128)S(1)} %convolution_add_fusion), kind=kOutput, calls=%fused_computation.49 | convolution fusion | flops 7248543744 | bytes 11796480 | tf_op jit(solution)/shard_map/dot_general | solution.py:86
  500.2 0.3 reduce-scatter.5.cloned.1.call-start
  500.4 427.3 %all-gather.29.cloned.1.call-done = f32[4096,3072]{1,0:T(8,128)} async-done(((f32[512,3072]{1,0:T(8,128)}), f32[4096,3072]{1,0:T(8,128)}) %all-gather.29.cloned.1.call-update) | async-done | bytes 50331664 | tf_op jit(solution)/shard_map/all_gather | solution.py:87
  927.8 21.2 %reduce_sum.97 = f32[512,3072]{1,0:T(8,128)} reduce(f32[8,512,3072]{2,1,0:T(8,128)} %bitcast.68, f32[]{:T(128)} %constant.202.clone.1), dimensions={0}, to_apply=%region_23.0 | reduce | flops 11010048 | bytes 56623108 | tf_op jit(solution)/shard_map/reduce_sum | solution.py:87
  949.0 12.7 %multiply_reduce_fusion.1 = (f32[]{:T(128)}, f32[512,3072]{1,0:T(8,128)}) fusion(f32[512,3072]{1,0:T(8,128)} %reduce_sum.97, f32[512,3072]{1,0:T(8,128)} %all-reduce.3.cloned.1.call-done, f32[512,3072]{1,0:T(8,128)} %all-gather.25.cloned.1.call-done), kind=kLoop, calls=%fused_computation.16 | loop fusion | flops 6291455 | bytes 25165828 | tf_op jit(solution)/shard_map/reduce_sum | solution.py:89
  961.7 11.3 %fusion = f32[384,3072]{1,0:T(8,128)} fusion(f32[512,3072]{1,0:T(8,128)} %get-tuple-element.745, f32[512,384]{1,0:T(8,128)S(1)} %convolution_add_fusion), kind=kOutput, calls=%fused_computation.20 | convolution fusion | flops 7250116608 | bytes 11796480 | tf_op jit(solution)/shard_map/dot_general | solution.py:91
  973.1 0.3 reduce-scatter.3.cloned.1.call-start
  973.4 14.1 %multiply_reduce_fusion.3 = (f32[384]{0:T(512)S(1)}, f32[512,384]{1,0:T(8,128)S(1)}) fusion(f32[512]{0:T(512)S(1)} %get-tuple-element.757, f32[512,384]{1,0:T(8,128)S(1)} %convolution_add_fusion, f32[384,3072]{1,0:T(8,128)} %param.21, f32[512,3072]{1,0:T(8,128)} %get-tuple-element.745), kind=kOutput, calls=%fused_computation.44 | convolution fusion | flops 7251295744 | bytes 12586496 | tf_op jit(solution)/shard_map/dot_general | solution.py:98
  987.4 15.4 %fusion.26 = f32[3072,384]{1,0:T(8,128)} fusion(f32[512,384]{1,0:T(8,128)S(1)} %get-tuple-element.761, f32[512,3072]{1,0:T(8,128)} %all-reduce.3.cloned.1.call-done, f32[512,3072]{1,0:T(8,128)} %all-gather.25.cloned.1.call-done, f32[512]{0:T(512)S(1)} %get-tuple-element.757, f32[512]{0:T(512)S(1)} %get-tuple-element.756), kind=kOutput, calls=%fused_computation.76 | convolution fusion | flops 7252475904 | bytes 18092032 | tf_op jit(solution)/shard_map/dot_general | solution.py:106
  1002.8 2.1 constant_dynamic-slice_fusion.6
  1004.9 10.4 all-reduce
  1016.0 12.5 %reduce-scatter.5.cloned.1.call-done = f32[384,768]{1,0:T(8,128)} async-done(((f32[384,3072]{1,0:T(8,128)}), f32[384,768]{1,0:T(8,128)}) %reduce-scatter.5.cloned.1.call-update) | async-done | bytes 1179664 | tf_op jit(solution)/shard_map/reduce_scatter | solution.py:112
  1028.4 60.4 %reduce-scatter.3.cloned.1.call-done = f32[768,384]{1,0:T(8,128)} async-done(((f32[3072,384]{1,0:T(8,128)}), f32[768,384]{1,0:T(8,128)}) %reduce-scatter.3.cloned.1.call-update) | async-done | bytes 1179664 | tf_op jit(solution)/shard_map/reduce_scatter | solution.py:111
  (106 shorter events, 1.4 us)
Async XLA Ops:
  7.2 69.9 %all-gather.25.cloned.1.call-start = ((), (), s32[]{:S(2)}) async-start(), calls=%async_computation.2 | async-start | bytes 7077888 | tf_op jit(solution)/shard_map/all_gather | solution.py:45
  7.9 165.9 %all-gather.27.cloned.1.call-start = ((), (), s32[]{:S(2)}) async-start(), calls=%async_computation.3 | async-start | bytes 11796480 | tf_op jit(solution)/shard_map/all_gather | solution.py:46
  8.6 464.9 %all-reduce.3.cloned.1.call-start = ((), (), s32[]{:S(2)}) async-start(), calls=%async_computation.4 | async-start | bytes 12582912 | tf_op jit(solution)/shard_map/psum | solution.py:75
  173.8 5.5 copy-start
  266.6 73.1 %copy-start.2 = (f32[512]{0:T(512)}, f32[512]{0:T(512)S(1)}, u32[]{:S(2)}) copy-start(f32[512]{0:T(512)S(1)} %add_subtract_fusion.2) | copy-start | bytes 6148
  293.9 45.8 %copy-start.1 = (f32[768]{0:T(1024)}, f32[768]{0:T(1024)S(1)}, u32[]{:S(2)}) copy-start(f32[768]{0:T(1024)S(1)} %add_subtract_fusion) | copy-start | bytes 9220
  339.7 0.7 copy-start.3
  339.7 133.8 %copy-start.4 = (f32[384]{0:T(512)S(1)}, f32[384]{0:T(512)}, u32[]{:S(2)}) copy-start(f32[384]{0:T(512)} %param.20) | copy-start | bytes 4612
  339.8 148.3 %slice-start = ((s8[4718592]{0:T(1024)(128)(4,1)}), s8[524288]{0:T(1024)(128)(4,1)S(1)}, s32[]{:S(2)}) async-start(s8[4718592]{0:T(1024)(128)(4,1)} %bitcast.69), calls=%async_computation.8 | async-start | bytes 1048576
  339.8 588.0 %all-gather.29.cloned.1.call-start = ((), (), s32[]{:S(2)}) async-start(), calls=%async_computation.7 | async-start | bytes 56623104 | tf_op jit(solution)/shard_map/all_gather | solution.py:87
  473.6 14.5 %slice-start.1 = ((s8[4718592]{0:T(1024)(128)(4,1)}), s8[4194304]{0:T(1024)(128)(4,1)S(1)}, s32[]{:S(2)}) async-start(s8[4718592]{0:T(1024)(128)(4,1)} %bitcast.69), calls=%async_computation.9 | async-start | bytes 8388608
  500.2 528.2 %reduce-scatter.5.cloned.1.call-start = ((), (), s32[]{:S(2)}) async-start(), calls=%async_computation.6 | async-start | bytes 5898240 | tf_op jit(solution)/shard_map/reduce_scatter | solution.py:112
  973.1 115.7 %reduce-scatter.3.cloned.1.call-start = ((), (), s32[]{:S(2)}) async-start(), calls=%async_computation.5 | async-start | bytes 5898240 | tf_op jit(solution)/shard_map/reduce_scatter | solution.py:111
Sparse Core Ops, SparseCore 0:
  9.6 67.4 all-gather.24
  78.9 94.8 all-gather.26
  339.9 133.6 all-reduce.2
  500.3 427.4 all-gather.28
  973.2 55.1 reduce-scatter.4
  1031.8 56.9 reduce-scatter.2
